TPU v7x, 256 devices: a whole 4x4x8 slice. The times are simulated.
256 devices in a mesh: scen: 16 (over z, x_lo), pt: 16 (over x_hi, y, core).
Axes of the slice: x: 4 (x_hi: 2, x_lo: 2; x = x_hi * 2 + x_lo), y: 4, z: 8, core: 2. Of those that a mesh axis runs over, the one named last changes fastest.
Arguments:
- slip_counts: int32 [2048, 2048], P('scen'), may hold values from 0 to 7
- spectra: bfloat16 [2048, 4, 4096], P('scen', None, 'pt'), may hold values from -0.125 to 0.125
- transfer: bfloat16 [4096, 4, 2048], P('pt', None, 'scen'), may hold values from -0.09375 to 0.09375
- coast_owner: int32 [2048], P('pt'), may hold values from 0 to 127
Outputs:
- coast: bfloat16 [2048, 4, 2048], P('scen', None, 'pt')
- region_energy: float32 [2048, 128], P('scen')
All inputs are finite; a program needn't handle non-finite values.
Results may differ from a plain program's by a relative error of at most 0.015.
Values may be sent and summed in bfloat16 or wider, within the bound.
A program may use at most 64 MiB of HBM per device.

v0:
```python
import jax
import jax.numpy as jnp
from jax import lax
from jax.sharding import PartitionSpec as P

C = 2048
REGIONS = 128
slip_step = 0.25


def coast_block(field_block, trans_block):
    outputs = []
    for freq in range(2):
        field_re = field_block[:, 2 * freq, :]
        field_im = field_block[:, 2 * freq + 1, :]
        real_left = jnp.stack([field_re, -field_im], axis=-1)
        imag_left = jnp.stack([field_im, field_re], axis=-1)
        left_both = jnp.stack([real_left, imag_left], axis=0)
        trans_pair = trans_block[:, 2 * freq : 2 * freq + 2, :]
        product = jnp.einsum(
            "xspc,pcd->sxd", left_both, trans_pair, preferred_element_type=jnp.float32
        )
        outputs.append(product)
    return jnp.concatenate(outputs, axis=1)


def per_device(slip_counts, spectra, transfer, coast_owner):
    weights = (slip_counts.astype(jnp.float32) * slip_step).astype(jnp.bfloat16)
    scen_rows = weights.shape[0]
    comps = spectra.shape[1]
    local_points = spectra.shape[2]
    piece = lax.all_gather(spectra, "scen", axis=0, tiled=True)
    flat_piece = piece.reshape(piece.shape[0], comps * local_points)
    field_sum = jnp.dot(weights, flat_piece, preferred_element_type=jnp.float32)
    field = field_sum.astype(jnp.bfloat16).reshape(scen_rows, comps, local_points)
    trans_whole = lax.all_gather(transfer, "scen", axis=2, tiled=True)
    partial_sum = coast_block(field, trans_whole)
    coast_sum = lax.psum_scatter(
        partial_sum.astype(jnp.bfloat16), "pt", scatter_dimension=2, tiled=True
    ).astype(jnp.float32)
    coast = coast_sum.astype(jnp.bfloat16)
    squares = jnp.sum(coast_sum * coast_sum, axis=1)
    onehot = (coast_owner[:, None] == jnp.arange(REGIONS, dtype=jnp.int32)[None, :]).astype(
        jnp.float32
    )
    local_energy = jnp.dot(
        squares, onehot, precision=lax.Precision.HIGHEST, preferred_element_type=jnp.float32
    )
    energy = lax.psum(local_energy.astype(jnp.bfloat16), "pt").astype(jnp.float32)
    return (coast, energy * (REGIONS / C))


def solution(mesh):
    placed = (P("scen", None), P("scen", None, "pt"), P("pt", None, "scen"), P("pt"))
    return jax.shard_map(
        per_device,
        mesh=mesh,
        in_specs=placed,
        out_specs=(P("scen", None, "pt"), P("scen", None)),
        check_vma=False,
    )
```

profile of v0, /device:TPU:32, one launch (start us, length us, event | category | flops | bytes accessed | tf_op | source)
XLA Modules:
  0.0 396.1 jit_solution(5593497343896343336)
XLA Ops:
  7.2 0.0 all-gather.3.cloned.1.call-start
  7.2 0.7 all-gather.3.cloned.1.call-update
  7.9 0.0 all-gather.5.cloned.1.call-start
  7.9 1.7 copy.14
  9.7 0.0 all-gather.5.cloned.1.call-update
  9.7 0.0 reduce-scatter.4.cloned.1.call-start
  9.7 101.5 %all-gather.3.cloned.1.call-done = bf16[2048,4,256]{2,1,0:T(4,128)(2,1)} async-done(((bf16[128,4,256]{2,1,0:T(4,128)(2,1)}), bf16[2048,4,256]{2,1,0:T(4,128)(2,1)}) %all-gather.3.cloned.1.call-update) | async-done | bytes 4194320 | tf_op jit(solution)/shard_map/all_gather | solution.py:32
  111.2 0.0 copy-start
  111.2 3.3 copy.27
  114.5 0.0 copy-done
  114.5 0.7 convolution_convert_fusion
  115.3 0.2 reshape.32
  115.4 0.4 fusion.17
  115.9 114.5 %all-gather.5.cloned.1.call-done = bf16[256,4,2048]{2,0,1:T(8,128)(2,1)} async-done(((bf16[256,4,128]{2,0,1:T(8,128)(2,1)}), bf16[256,4,2048]{2,0,1:T(8,128)(2,1)}) %all-gather.5.cloned.1.call-update) | async-done | bytes 4194320 | tf_op jit(solution)/shard_map/all_gather | solution.py:36
  230.4 2.3 fusion.3
  232.7 2.3 fusion.2
  235.0 0.2 pad_maximum_fusion
  235.2 2.5 copy.20
  237.8 3.3 copy.36
  241.1 0.0 copy-start.1
  241.1 0.0 reduce-scatter.4.cloned.1.call-update
  241.1 80.7 %reduce-scatter.4.cloned.1.call-done = bf16[128,512]{1,0:T(8,128)(2,1)} async-done(((bf16[2048,512]{1,0:T(8,128)(2,1)}), bf16[128,512]{1,0:T(8,128)(2,1)}) %reduce-scatter.4.cloned.1.call-update) | async-done | bytes 131088
  321.8 0.9 reshape.38
  322.7 0.8 copy.17
  323.5 0.1 copy.21
  323.7 0.0 copy-done.1
  323.7 0.2 convolution_convert_fusion.1
  324.0 65.0 %psum.7 = bf16[128,128]{1,0:T(8,128)(2,1)S(1)} all-reduce(bf16[128,128]{1,0:T(8,128)(2,1)S(1)} %convolution_convert_fusion.1), channel_id=1, replica_groups=mesh['scen'=16,'pt'=16] {'pt'}, use_global_device_ids=true, to_apply=%region_2.0 | all-reduce | flops 16384 | bytes 65536 | tf_op jit(solution)/shard_map/psum | solution.py:49
  388.9 0.6 convert_multiply_fusion
  (5 shorter events, 0.1 us)
Async XLA Ops:
  7.2 104.0 %all-gather.3.cloned.1.call-start = ((), (), s32[]{:S(2)}) async-start(), calls=%async_computation.1 | async-start | bytes 4456448 | tf_op jit(solution)/shard_map/all_gather | solution.py:32
  7.9 222.5 %all-gather.5.cloned.1.call-start = ((), (), s32[]{:S(2)}) async-start(), calls=%async_computation.2 | async-start | bytes 4456448 | tf_op jit(solution)/shard_map/all_gather | solution.py:36
  9.7 312.1 %reduce-scatter.4.cloned.1.call-start = ((), (), s32[]{:S(2)}) async-start(), calls=%async_computation.3 | async-start | bytes 2228224
  111.2 3.3 copy-start
  241.1 82.7 %copy-start.1 = (s32[128]{0:T(128)S(1)}, s32[128]{0:T(128)}, u32[]{:S(2)}) copy-start(s32[128]{0:T(128)} %param.7) | copy-start | bytes 1540
Sparse Core Ops, SparseCore 0:
  9.8 101.3 all-gather.2
  112.9 117.4 all-gather.4
  241.2 80.5 reduce-scatter.3
where the time goes:
time: 396 us
  waiting for transfers between devices  297 us (75%)
  blocking collectives  65 us (16%)
  between operations  13.9 us (4%)
  local copies, waits for them, and re-layouts  13.3 us (3%)
  matrix products  5.58 us (1%)
    all_gather x1, waiting for transfers between devices, per_device(): trans_whole = lax.all_gather(transfer, 'scen', axis=2, tiled=True)  114 us
    all_gather x1, waiting for transfers between devices, per_device(): piece = lax.all_gather(spectra, 'scen', axis=0, tiled=True)  101 us
    unnamed x4, waiting for transfers between devices  81.4 us
    psum x1, blocking collectives, per_device(): lax.psum(local_energy.astype(jnp.bfloat16), 'pt').astype(jnp.float32)  65 us
    unnamed x11, local copies, waits for them, and re-layouts  12.7 us
  transfers between devices with their start and end apart: 3, of which 3 were waited for; matrix products, arithmetic and copies ran while one was open for 2% of the time, Pallas kernels for 0%

commit v1 on v0

--- a/solution.py
+++ b/solution.py
@@ -46,7 +46,9 @@
     local_energy = jnp.dot(
         squares, onehot, precision=lax.Precision.HIGHEST, preferred_element_type=jnp.float32
     )
-    energy = lax.psum(local_energy.astype(jnp.bfloat16), "pt").astype(jnp.float32)
+    energy = jnp.sum(lax.all_gather(local_energy.astype(jnp.bfloat16), "pt"), axis=0).astype(
+        jnp.float32
+    )
     return (coast, energy * (REGIONS / C))
 
 

time: 396 us -> 356 us (0.90)
  blocking collectives: 65 us -> 22.9 us
    psum x1 -> x0, blocking collectives: 65 us -> none  [per_device(): lax.psum(local_energy.astype(jnp.bfloat16), 'pt').astype(jnp.float32)]
    all_gather x0 -> x1, blocking collectives: none -> 22.9 us  [per_device(): lax.all_gather(local_energy.astype(jnp.bfloat16), 'pt')]
where the time goes in v1:
time: 356 us; the launch traced here: 354 us
  waiting for transfers between devices  297 us (83%)
  blocking collectives  22.9 us (6%)
  between operations  13.9 us (4%)
  local copies, waits for them, and re-layouts  13.3 us (4%)
  matrix products  5.58 us (2%)
    all_gather x1, waiting for transfers between devices, per_device(): trans_whole = lax.all_gather(transfer, 'scen', axis=2, tiled=True)  114 us
    all_gather x1, waiting for transfers between devices, per_device(): piece = lax.all_gather(spectra, 'scen', axis=0, tiled=True)  101 us
    unnamed x4, waiting for transfers between devices  81.4 us
    all_gather x1, blocking collectives, per_device(): lax.all_gather(local_energy.astype(jnp.bfloat16), 'pt')  22.9 us
    unnamed x11, local copies, waits for them, and re-layouts  12.7 us
  transfers between devices with their start and end apart: 3, of which 3 were waited for; matrix products, arithmetic and copies ran while one was open for 2% of the time, Pallas kernels for 0%

profile of v1, /device:TPU:32, one launch (start us, length us, event | category | flops | bytes accessed | tf_op | source)
XLA Modules:
  0.0 354.1 jit_solution(9042144400755292072)
XLA Ops:
  7.2 0.0 all-gather.4.cloned.1.call-start
  7.2 0.7 all-gather.4.cloned.1.call-update
  7.9 0.0 all-gather.6.cloned.1.call-start
  7.9 1.7 copy.14
  9.7 0.0 all-gather.6.cloned.1.call-update
  9.7 0.0 reduce-scatter.4.cloned.1.call-start
  9.7 101.5 %all-gather.4.cloned.1.call-done = bf16[2048,4,256]{2,1,0:T(4,128)(2,1)} async-done(((bf16[128,4,256]{2,1,0:T(4,128)(2,1)}), bf16[2048,4,256]{2,1,0:T(4,128)(2,1)}) %all-gather.4.cloned.1.call-update) | async-done | bytes 4194320 | tf_op jit(solution)/shard_map/all_gather | solution.py:32
  111.2 0.0 copy-start
  111.2 3.3 copy.27
  114.5 0.0 copy-done
  114.5 0.7 convolution_convert_fusion
  115.3 0.2 reshape.32
  115.4 0.4 fusion.17
  115.9 114.5 %all-gather.6.cloned.1.call-done = bf16[256,4,2048]{2,0,1:T(8,128)(2,1)} async-done(((bf16[256,4,128]{2,0,1:T(8,128)(2,1)}), bf16[256,4,2048]{2,0,1:T(8,128)(2,1)}) %all-gather.6.cloned.1.call-update) | async-done | bytes 4194320 | tf_op jit(solution)/shard_map/all_gather | solution.py:36
  230.4 2.3 fusion.3
  232.7 2.3 fusion.2
  235.0 0.2 pad_maximum_fusion
  235.2 2.5 copy.20
  237.8 3.3 copy.36
  241.1 0.0 copy-start.1
  241.1 0.0 reduce-scatter.4.cloned.1.call-update
  241.1 80.7 %reduce-scatter.4.cloned.1.call-done = bf16[128,512]{1,0:T(8,128)(2,1)} async-done(((bf16[2048,512]{1,0:T(8,128)(2,1)}), bf16[128,512]{1,0:T(8,128)(2,1)}) %reduce-scatter.4.cloned.1.call-update) | async-done | bytes 131088
  321.8 0.9 reshape.39
  322.7 0.8 copy.17
  323.5 0.1 copy.21
  323.7 0.0 copy-done.1
  323.7 0.2 convolution_convert_fusion.1
  324.0 22.9 %all-gather = bf16[2048,128]{1,0:T(8,128)(2,1)S(1)} all-gather(bf16[128,128]{1,0:T(8,128)(2,1)S(1)} %convolution_convert_fusion.1), channel_id=2, replica_groups=mesh['scen'=16,'pt'=16] {'pt'}, dimensions={0}, use_global_device_ids=true | all-gather | bytes 557056 | tf_op jit(solution)/shard_map/all_gather | solution.py:49
  346.9 0.1 reduce_sum.22
  347.0 0.6 convert_multiply_fusion
  (5 shorter events, 0.1 us)
Async XLA Ops:
  7.2 104.0 %all-gather.4.cloned.1.call-start = ((), (), s32[]{:S(2)}) async-start(), calls=%async_computation.1 | async-start | bytes 4456448 | tf_op jit(solution)/shard_map/all_gather | solution.py:32
  7.9 222.5 %all-gather.6.cloned.1.call-start = ((), (), s32[]{:S(2)}) async-start(), calls=%async_computation.2 | async-start | bytes 4456448 | tf_op jit(solution)/shard_map/all_gather | solution.py:36
  9.7 312.1 %reduce-scatter.4.cloned.1.call-start = ((), (), s32[]{:S(2)}) async-start(), calls=%async_computation.3 | async-start | bytes 2228224
  111.2 3.3 copy-start
  241.1 82.7 %copy-start.1 = (s32[128]{0:T(128)S(1)}, s32[128]{0:T(128)}, u32[]{:S(2)}) copy-start(s32[128]{0:T(128)} %param.7) | copy-start | bytes 1540
Sparse Core Ops, SparseCore 0:
  9.8 101.3 all-gather.3
  112.9 117.4 all-gather.5
  241.2 80.5 reduce-scatter.3

commit v2 on v0

--- a/solution.py
+++ b/solution.py
@@ -33,7 +33,9 @@
     flat_piece = piece.reshape(piece.shape[0], comps * local_points)
     field_sum = jnp.dot(weights, flat_piece, preferred_element_type=jnp.float32)
     field = field_sum.astype(jnp.bfloat16).reshape(scen_rows, comps, local_points)
-    trans_whole = lax.all_gather(transfer, "scen", axis=2, tiled=True)
+    trans_whole = jnp.concatenate(
+        lax.all_to_all(jnp.stack([transfer] * lax.axis_size("scen")), "scen", 0, 0), axis=2
+    )
     partial_sum = coast_block(field, trans_whole)
     coast_sum = lax.psum_scatter(
         partial_sum.astype(jnp.bfloat16), "pt", scatter_dimension=2, tiled=True

time: 396 us -> 349 us (0.88)
  waiting for transfers between devices: 297 us -> 238 us
  starting transfers between devices: 0.12 us -> 9.59 us
  local copies, waits for them, and re-layouts: 13.3 us -> 18.4 us
    all_gather x1 -> x0, waiting for transfers between devices: 114 us -> none  [per_device(): trans_whole = lax.all_gather(transfer, 'scen', axis=2, tiled=True)]
    all_gather x1, waiting for transfers between devices: 101 us -> 158 us  [per_device(): piece = lax.all_gather(spectra, 'scen', axis=0, tiled=True)]
    all_to_all x0 -> x1, starting transfers between devices: none -> 9.51 us  [per_device(): lax.all_to_all(jnp.stack([transfer] * lax.axis_size('scen')), 'scen', 0, 0)]
    unnamed x4 -> x3, waiting for transfers between devices: 81.4 us -> 79.8 us
  transfers between devices with their start and end apart: 3 -> 3, of which waited for: 3 -> 2; matrix products, arithmetic and copies ran while one was open for 2% -> 2% of each run, Pallas kernels for 0% -> 0%
where the time goes in v2:
time: 349 us
  waiting for transfers between devices  238 us (68%)
  blocking collectives  65 us (19%)
  local copies, waits for them, and re-layouts  18.4 us (5%)
  between operations  14.2 us (4%)
  starting transfers between devices  9.59 us (3%)
    all_gather x1, waiting for transfers between devices, per_device(): piece = lax.all_gather(spectra, 'scen', axis=0, tiled=True)  158 us
    unnamed x3, waiting for transfers between devices  79.8 us
    psum x1, blocking collectives, per_device(): lax.psum(local_energy.astype(jnp.bfloat16), 'pt').astype(jnp.float32)  65 us
    unnamed x11, local copies, waits for them, and re-layouts  12.1 us
    all_to_all x1, starting transfers between devices, per_device(): lax.all_to_all(jnp.stack([transfer] * lax.axis_size('scen')), 'scen', 0, 0)  9.51 us
  transfers between devices with their start and end apart: 3, of which 2 were waited for; matrix products, arithmetic and copies ran while one was open for 2% of the time, Pallas kernels for 0%

profile of v2, /device:TPU:32, one launch (start us, length us, event | category | flops | bytes accessed | tf_op | source)
XLA Modules:
  0.0 348.6 jit_solution(11369902358301048861)
XLA Ops:
  7.2 0.0 all-gather.2.cloned.1.call-start
  7.2 0.7 all-gather.2.cloned.1.call-update
  7.9 1.0 copy.14
  8.9 3.0 stack.27
  11.9 9.5 %all-to-all-start = ((bf16[16,256,4,128]{3,1,2,0:T(8,128)(2,1)}), bf16[16,256,4,128]{3,1,2,0:T(8,128)(2,1)}, u32[]{:S(2)}, u32[]{:S(2)}) async-start(bf16[16,256,4,128]{3,1,2,0:T(8,128)(2,1)} %stack.27), calls=%async_computation | async-start | bytes 8388608 | tf_op jit(solution)/shard_map/all_to_all | solution.py:37
  21.4 0.0 reduce-scatter.4.cloned.1.call-start
  21.4 158.3 %all-gather.2.cloned.1.call-done = bf16[2048,4,256]{2,1,0:T(4,128)(2,1)} async-done(((bf16[128,4,256]{2,1,0:T(4,128)(2,1)}), bf16[2048,4,256]{2,1,0:T(4,128)(2,1)}) %all-gather.2.cloned.1.call-update) | async-done | bytes 4194320 | tf_op jit(solution)/shard_map/all_gather | solution.py:32
  179.8 0.0 copy-start
  179.8 3.3 copy.29
  183.1 0.0 copy-done
  183.1 0.7 convolution_convert_fusion
  183.8 0.2 reshape.40
  184.0 0.4 fusion.17
  184.5 0.0 all-to-all-done
  184.5 2.8 copy_bitcast_fusion
  187.3 0.7 fusion.3
  188.1 0.7 fusion.2
  188.8 0.2 pad_maximum_fusion
  189.0 2.6 copy.21
  191.6 0.0 copy-start.1
  191.6 3.3 copy.39
  194.9 0.0 reduce-scatter.4.cloned.1.call-update
  194.9 79.1 %reduce-scatter.4.cloned.1.call-done = bf16[128,512]{1,0:T(8,128)(2,1)} async-done(((bf16[2048,512]{1,0:T(8,128)(2,1)}), bf16[128,512]{1,0:T(8,128)(2,1)}) %reduce-scatter.4.cloned.1.call-update) | async-done | bytes 131088
  274.0 0.9 reshape.48
  275.0 0.1 copy.22
  275.1 0.8 copy.18
  275.9 0.0 copy-done.1
  276.0 0.2 convolution_convert_fusion.1
  276.2 65.0 %psum.7 = bf16[128,128]{1,0:T(8,128)(2,1)S(1)} all-reduce(bf16[128,128]{1,0:T(8,128)(2,1)S(1)} %convolution_convert_fusion.1), channel_id=1, replica_groups=mesh['scen'=16,'pt'=16] {'pt'}, use_global_device_ids=true, to_apply=%region_2.0 | all-reduce | flops 16384 | bytes 65536 | tf_op jit(solution)/shard_map/psum | solution.py:51
  341.2 0.6 convert_multiply_fusion
  (5 shorter events, 0.1 us)
Async XLA Ops:
  7.2 172.6 %all-gather.2.cloned.1.call-start = ((), (), s32[]{:S(2)}) async-start(), calls=%async_computation.2 | async-start | bytes 4456448 | tf_op jit(solution)/shard_map/all_gather | solution.py:32
  11.9 172.6 %all-to-all-start = ((bf16[16,256,4,128]{3,1,2,0:T(8,128)(2,1)}), bf16[16,256,4,128]{3,1,2,0:T(8,128)(2,1)}, u32[]{:S(2)}, u32[]{:S(2)}) async-start(bf16[16,256,4,128]{3,1,2,0:T(8,128)(2,1)} %stack.27), calls=%async_computation | async-start | bytes 8388608 | tf_op jit(solution)/shard_map/all_to_all | solution.py:37
  21.4 252.6 %reduce-scatter.4.cloned.1.call-start = ((), (), s32[]{:S(2)}) async-start(), calls=%async_computation.3 | async-start | bytes 2228224
  179.8 3.3 copy-start
  191.6 84.4 %copy-start.1 = (s32[128]{0:T(128)S(1)}, s32[128]{0:T(128)}, u32[]{:S(2)}) copy-start(s32[128]{0:T(128)} %param.7) | copy-start | bytes 1540
Sparse Core Ops, SparseCore 0:
  9.8 169.9 all-gather.1
  195.0 78.9 reduce-scatter.3
